TPU v7x, 256 devices: a whole 4x4x8 slice. The times are simulated.
256 devices in a mesh: frame: 8 (over z), tile: 32 (over x, y, core).
Axes of the slice: x: 4, y: 4, z: 8, core: 2. Of those that a mesh axis runs over, the one named last changes fastest.
Arguments:
- displacement: bfloat16 [512, 2, 32, 4096], P('frame', None, 'tile'), may hold values from -256 to 256
Outputs:
- basis: bfloat16 [512, 3, 32, 4096], P(None, None, 'tile', 'frame')
- factor: float32 [512, 512], replicated
All inputs are finite; a program needn't handle non-finite values.
Results may differ from a plain program's by a relative error of at most 0.0053.
The roundings to bfloat16 on the way count: a program that leaves them out, or rounds other values in their place, can miss the bound.
Values may be sent and summed in bfloat16 or wider, within the bound.
No kernel may reach another device: no remote copies, remote signals or barrier semaphores. Data moves between devices by JAX's collectives and lax.ppermute only.
A program may use at most 64 MiB of HBM per device.

v0:
```python
import math
import jax
import jax.numpy as jnp
from jax import lax
from jax.sharding import PartitionSpec as P


def with_halo(array, sides, width):
    for axis, dim in sides:
        peers, length = (lax.axis_size(axis), array.shape[dim])
        up = [(i, (i + 1) % peers) for i in range(peers - 1)]
        down = [(j, i) for i, j in up]
        last = lax.slice_in_dim(array, length - width, length, axis=dim)
        first = lax.slice_in_dim(array, 0, width, axis=dim)
        before = lax.ppermute(last, axis, up)
        after = lax.ppermute(first, axis, down)
        array = jnp.concatenate([before, array, after], axis=dim)
    return array


def derivative(center, before, after, first, final):
    return jnp.where(
        first, after - center, jnp.where(final, center - before, (after - before) * 0.5)
    )


def column_derivative(center):
    width = center.shape[-1]
    after = jnp.concatenate([center[..., 1:], center[..., -1:]], axis=-1)
    before = jnp.concatenate([center[..., :1], center[..., :-1]], axis=-1)
    column = jnp.arange(width, dtype=jnp.int32)
    return derivative(center, before, after, column == 0, column == width - 1)


def combine_strain(d_rows, d_cols):
    return jnp.stack(
        [d_cols[:, 0], d_rows[:, 1], 0.5 * (d_rows[:, 0] + d_cols[:, 1])], axis=1
    ).astype(jnp.bfloat16)


def local(displacement):
    rows = displacement.shape[2]
    full_width = displacement.shape[3]
    total_rows = lax.axis_size("tile") * rows
    scale = math.sqrt(3 * total_rows * full_width)
    row_global = lax.axis_index("tile") * rows + jnp.arange(rows, dtype=jnp.int32)
    first = (row_global == 0)[:, None]
    final = (row_global == total_rows - 1)[:, None]
    padded = with_halo(displacement, (("tile", 2),), 1)
    field = padded.astype(jnp.float32)
    center = field[:, :, 1:-1, :]
    d_rows = derivative(center, field[:, :, :-2, :], field[:, :, 2:, :], first, final)
    d_cols = column_derivative(center)
    strain = combine_strain(d_rows, d_cols)
    pixel_major = lax.all_to_all(strain, "frame", split_axis=3, concat_axis=0, tiled=True)
    frames = pixel_major.shape[0]
    snapshot_half = pixel_major.reshape(frames, -1)
    local_gram = lax.dot_general(
        snapshot_half, snapshot_half, (((1,), (1,)), ((), ())), preferred_element_type=jnp.float32
    )
    gram = lax.psum(local_gram, ("frame", "tile"))
    lower = jnp.linalg.cholesky(gram)
    snapshot = snapshot_half.astype(jnp.float32)
    solved = lax.linalg.triangular_solve(lower, snapshot, left_side=True, lower=True)
    basis = (solved * scale).astype(jnp.bfloat16).reshape(pixel_major.shape)
    return (basis, lower.T / scale)


def solution(mesh):
    return jax.shard_map(
        local,
        mesh=mesh,
        in_specs=(P("frame", None, "tile", None),),
        out_specs=(P(None, None, "tile", "frame"), P()),
        check_vma=False,
    )
```

profile of v0, /device:TPU:2, one launch (start us, length us, event | category | flops | bytes accessed | tf_op | source)
XLA Modules:
  0.0 526.9 jit_solution(18431249091505621572)
XLA Ops:
  7.2 1.8 copy.46
  9.0 1.9 collective-permute-start
  10.9 5.8 %collective-permute-start.1 = (bf16[64,2,1,4096]{3,0,2,1:T(8,128)(2,1)S(1)}, bf16[64,2,1,4096]{3,0,2,1:T(8,128)(2,1)S(1)}, u32[]{:S(2)}, u32[]{:S(2)}) collective-permute-start(bf16[64,2,1,4096]{3,0,2,1:T(8,128)(2,1)S(1)} %copy.46), channel_id=1, source_target_pairs={{1,0},{2,1},{3,2},{4,3},{5,4},{6,5},{7,6},{8,7},{9,8},{10,9},{11,1... | collective-permute-start | bytes 3145736 | tf_op jit(solution)/shard_map/ppermute | solution.py:16
  16.7 10.5 %collective-permute-done = bf16[64,2,1,4096]{3,0,2,1:T(8,128)(2,1)S(1)} collective-permute-done((bf16[64,2,1,4096]{3,0,2,1:T(8,128)(2,1)S(1)}, bf16[64,2,1,4096]{3,0,2,1:T(8,128)(2,1)S(1)}, u32[]{:S(2)}, u32[]{:S(2)}) %collective-permute-start) | collective-permute-done | bytes 1048608 | tf_op jit(solution)/shard_map/ppermute | solution.py:15
  27.2 1.8 collective-permute-done.1
  32.2 4.7 copy.49
  36.9 6.1 %reshape.243 = bf16[8,2,49152]{2,1,0:T(2,128)(2,1)S(1)} reshape(bf16[4096,1,3,64]{3,2,1,0:T(4,128)(2,1)} %bitcast.77) | data formatting | bytes 3145728
  43.0 48.1 %all_to_all.15 = bf16[8,2,49152]{2,1,0:T(2,128)(2,1)S(1)} all-to-all(bf16[8,2,49152]{2,1,0:T(2,128)(2,1)S(1)} %reshape.243), channel_id=1, replica_groups=mesh['frame'=8,'tile'=32] {'frame'}, dimensions={0} | all-to-all | bytes 3145728 | tf_op jit(solution)/shard_map/all_to_all | solution.py:55
  91.2 4.8 reshape.244
  96.0 4.8 copy.67
  102.7 2.0 fusion.36
  104.9 2.1 convert_element_type.26
  108.2 248.2 %all-reduce.3.cloned.1.call-done = f32[512,512]{0,1:T(8,128)} async-done(((f32[512,512]{0,1:T(8,128)}), f32[512,512]{0,1:T(8,128)}) %all-reduce.3.cloned.1.call-update) | async-done | bytes 1048592 | tf_op jit(solution)/shard_map/psum | solution.py:61
  358.3 11.7 %cholesky.104 = f32[128,128]{1,0:T(8,128)S(1)} custom-call(f32[128,128]{1,0:T(8,128)S(1)} %cholesky.266), custom_call_target="Cholesky" | custom-call | tf_op jit(solution)/shard_map/jit(cholesky)/cholesky | solution.py:62
  370.2 9.8 %custom-call.30 = f32[1,128,128]{1,2,0:T(8,128)S(1)} custom-call(f32[1,128,128]{2,1,0:T(8,128)S(1)} %get-tuple-element.45), custom_call_target="InvertDiagBlocksLowerTriangular" | custom-call | tf_op jit(solution)/shard_map/jit(cholesky)/cholesky | solution.py:62
  380.7 11.8 %cholesky.217 = f32[128,128]{1,0:T(8,128)S(1)} custom-call(f32[128,128]{1,0:T(8,128)S(1)} %cholesky.270), custom_call_target="Cholesky" | custom-call | tf_op jit(solution)/shard_map/jit(cholesky)/cholesky | solution.py:62
  393.8 9.8 %custom-call.31 = f32[1,128,128]{1,2,0:T(8,128)S(1)} custom-call(f32[1,128,128]{2,1,0:T(8,128)S(1)} %get-tuple-element.42), custom_call_target="InvertDiagBlocksLowerTriangular" | custom-call | tf_op jit(solution)/shard_map/jit(cholesky)/cholesky | solution.py:62
  404.3 11.7 %cholesky.238 = f32[128,128]{1,0:T(8,128)S(1)} custom-call(f32[128,128]{1,0:T(8,128)S(1)} %cholesky.275), custom_call_target="Cholesky" | custom-call | tf_op jit(solution)/shard_map/jit(cholesky)/cholesky | solution.py:62
  416.7 9.8 %custom-call.32 = f32[1,128,128]{1,2,0:T(8,128)S(1)} custom-call(f32[1,128,128]{2,1,0:T(8,128)S(1)} %get-tuple-element.39), custom_call_target="InvertDiagBlocksLowerTriangular" | custom-call | tf_op jit(solution)/shard_map/jit(cholesky)/cholesky | solution.py:62
  427.1 11.9 %cholesky.255 = f32[128,128]{1,0:T(8,128)S(1)} custom-call(f32[128,128]{1,0:T(8,128)S(1)} %convolution_subtract_fusion.5), custom_call_target="Cholesky" | custom-call | tf_op jit(solution)/shard_map/jit(cholesky)/cholesky | solution.py:62
  442.6 10.0 %while.1 = (s32[]{:T(128)}, f32[512,512]{1,0:T(8,128)S(1)}, s32[4,2]{0,1:T(2,128)S(1)}, f32[4,128,128]{2,1,0:T(8,128)}, s32[]{:T(128)}) while((s32[]{:T(128)}, f32[512,512]{1,0:T(8,128)S(1)}, s32[4,2]{0,1:T(2,128)S(1)}, f32[4,128,128]{2,1,0:T(8,128)}, s32[]{:T(128)}) %tuple.39), condition=%wide.while_cond, body=%wide.while_body.sunk | while | flops 2 | bytes 132705 | solution.py:64
  443.2 1.9 bitcast_dynamic-update-slice_fusion.2
  445.7 1.9 bitcast_dynamic-update-slice_fusion.2
  448.2 1.9 bitcast_dynamic-update-slice_fusion.2
  450.7 1.9 bitcast_dynamic-update-slice_fusion.2
  452.6 40.2 %custom-call.33 = f32[4,128,128]{1,2,0:T(8,128)S(1)} custom-call(f32[4,128,128]{2,1,0:T(8,128)} %get-tuple-element.9), custom_call_target="InvertDiagBlocksLowerTriangular" | custom-call | tf_op jit(solution)/shard_map/triangular_solve | solution.py:64
  494.4 2.1 convolution_subtract_fusion.2
  498.3 1.9 convolution_subtract_fusion
  501.9 3.4 fusion.1
  510.1 1.7 convolution_bitcast_fusion
  513.5 2.3 copy.60
  517.1 2.7 fusion.7
  (68 shorter events, 28.6 us)
Async XLA Ops:
  7.2 349.3 %all-reduce.3.cloned.1.call-start = ((), (), s32[]{:S(2)}) async-start(), calls=%async_computation.1 | async-start | bytes 2097152 | tf_op jit(solution)/shard_map/psum | solution.py:61
  9.0 18.2 %collective-permute-start = (bf16[64,2,1,4096]{3,0,2,1:T(8,128)(2,1)S(1)}, bf16[64,2,1,4096]{3,0,2,1:T(8,128)(2,1)S(1)}, u32[]{:S(2)}, u32[]{:S(2)}) collective-permute-start(bf16[64,2,1,4096]{3,0,2,1:T(8,128)(2,1)S(1)} %copy.46), channel_id=1, source_target_pairs={{0,1},{1,2},{2,3},{3,4},{4,5},{5,6},{6,7},{7,8},{8,9},{9,10},{10,1... | collective-permute-start | bytes 3145736 | tf_op jit(solution)/shard_map/ppermute | solution.py:15
  10.9 18.1 %collective-permute-start.1 = (bf16[64,2,1,4096]{3,0,2,1:T(8,128)(2,1)S(1)}, bf16[64,2,1,4096]{3,0,2,1:T(8,128)(2,1)S(1)}, u32[]{:S(2)}, u32[]{:S(2)}) collective-permute-start(bf16[64,2,1,4096]{3,0,2,1:T(8,128)(2,1)S(1)} %copy.46), channel_id=1, source_target_pairs={{1,0},{2,1},{3,2},{4,3},{5,4},{6,5},{7,6},{8,7},{9,8},{10,9},{11,1... | collective-permute-start | bytes 3145736 | tf_op jit(solution)/shard_map/ppermute | solution.py:16
  356.4 1.7 copy-start.1
  452.6 40.2 %copy-start.3 = (f32[512,512]{1,0:T(8,128)}, f32[512,512]{1,0:T(8,128)S(1)}, u32[]{:S(2)}) copy-start(f32[512,512]{1,0:T(8,128)S(1)} %get-tuple-element.100) | copy-start | bytes 3145732
  492.8 1.6 copy-start.4
  494.4 3.8 copy-start
  507.6 4.3 copy-start.2
Sparse Core Ops, SparseCore 0:
  104.8 251.5 all-reduce.2
where the time goes:
time: 532 us; the launch traced here: 527 us
  waiting for transfers between devices  261 us (49%)
  other arithmetic  127 us (24%)
  local copies, waits for them, and re-layouts  48.3 us (9%)
  blocking collectives  48.1 us (9%)
  matrix products  17.9 us (3%)
  between operations  17.2 us (3%)
  starting transfers between devices  7.71 us (1%)
    psum x1, waiting for transfers between devices, local(): gram = lax.psum(local_gram, ('frame', 'tile'))  248 us
    another operation x15, other arithmetic, local(): lower = jnp.linalg.cholesky(gram)  79.4 us
    all_to_all x1, blocking collectives, local(): lax.all_to_all(strain, 'frame', split_axis=3, concat_axis=0, tiled=True)  48.1 us
    another operation x2, other arithmetic, local(): lax.linalg.triangular_solve(lower, snapshot, left_side=True, lower=True)  40.2 us
    unnamed x16, local copies, waits for them, and re-layouts  15.4 us
    another operation x7, matrix products, local(): lax.linalg.triangular_solve(lower, snapshot, left_side=True, lower=True)  14.1 us
  transfers between devices with their start and end apart: 3, of which 3 were waited for; matrix products, arithmetic and copies ran while one was open for 1% of the time, Pallas kernels for 0%

commit v1 on v0

--- a/solution.py
+++ b/solution.py
@@ -1,8 +1,16 @@
+import functools
 import math
 import jax
 import jax.numpy as jnp
 from jax import lax
 from jax.sharding import PartitionSpec as P
+
+
+def remake_wires(frame, mesh_name, group_axis):
+    return jax.lax.psum(jax.lax.psum(frame, mesh_name), group_axis)
+
+
+unite_the_stops_all = functools.partial(remake_wires, mesh_name="tile", group_axis="frame")
 
 
 def with_halo(array, sides, width):
@@ -58,7 +66,7 @@
     local_gram = lax.dot_general(
         snapshot_half, snapshot_half, (((1,), (1,)), ((), ())), preferred_element_type=jnp.float32
     )
-    gram = lax.psum(local_gram, ("frame", "tile"))
+    gram = unite_the_stops_all(local_gram)
     lower = jnp.linalg.cholesky(gram)
     snapshot = snapshot_half.astype(jnp.float32)
     solved = lax.linalg.triangular_solve(lower, snapshot, left_side=True, lower=True)

time: 532 us -> 471 us (0.89)
  waiting for transfers between devices: 261 us -> 197 us
    psum x1 -> x2, waiting for transfers between devices: 248 us -> 185 us  [remake_wires(): return jax.lax.psum(jax.lax.psum(frame, mesh_name), group_axis)]
  transfers between devices with their start and end apart: 3 -> 4, of which waited for: 3 -> 4; matrix products, arithmetic and copies ran while one was open for 1% -> 1% of each run, Pallas kernels for 0% -> 0%
where the time goes in v1:
time: 471 us; the launch traced here: 464 us
  waiting for transfers between devices  197 us (42%)
  other arithmetic  127 us (27%)
  blocking collectives  48.1 us (10%)
  local copies, waits for them, and re-layouts  47.8 us (10%)
  matrix products  17.9 us (4%)
  between operations  17.2 us (4%)
  starting transfers between devices  8.22 us (2%)
    psum x2, waiting for transfers between devices, remake_wires(): return jax.lax.psum(jax.lax.psum(frame, mesh_name), group_axis)  185 us
    another operation x15, other arithmetic, local(): lower = jnp.linalg.cholesky(gram)  79.4 us
    all_to_all x1, blocking collectives, local(): lax.all_to_all(strain, 'frame', split_axis=3, concat_axis=0, tiled=True)  48.1 us
    another operation x2, other arithmetic, local(): lax.linalg.triangular_solve(lower, snapshot, left_side=True, lower=True)  40.2 us
    unnamed x16, local copies, waits for them, and re-layouts  15.4 us
    another operation x7, matrix products, local(): lax.linalg.triangular_solve(lower, snapshot, left_side=True, lower=True)  14.1 us
    ppermute x1, waiting for transfers between devices, with_halo(): before = lax.ppermute(last, axis, up)  10.5 us
    another operation x12, local copies, waits for them, and re-layouts  9.98 us
  transfers between devices with their start and end apart: 4, of which 4 were waited for; matrix products, arithmetic and copies ran while one was open for 1% of the time, Pallas kernels for 0%

profile of v1, /device:TPU:2, one launch (start us, length us, event | category | flops | bytes accessed | tf_op | source)
XLA Modules:
  0.0 463.6 jit_solution(6460907395932185622)
XLA Ops:
  7.2 1.8 copy.46
  9.0 1.9 collective-permute-start
  10.9 5.8 %collective-permute-start.1 = (bf16[64,2,1,4096]{3,0,2,1:T(8,128)(2,1)S(1)}, bf16[64,2,1,4096]{3,0,2,1:T(8,128)(2,1)S(1)}, u32[]{:S(2)}, u32[]{:S(2)}) collective-permute-start(bf16[64,2,1,4096]{3,0,2,1:T(8,128)(2,1)S(1)} %copy.46), channel_id=1, source_target_pairs={{1,0},{2,1},{3,2},{4,3},{5,4},{6,5},{7,6},{8,7},{9,8},{10,9},{11,1... | collective-permute-start | bytes 3145736 | tf_op jit(solution)/shard_map/ppermute | solution.py:24
  16.7 10.5 %collective-permute-done = bf16[64,2,1,4096]{3,0,2,1:T(8,128)(2,1)S(1)} collective-permute-done((bf16[64,2,1,4096]{3,0,2,1:T(8,128)(2,1)S(1)}, bf16[64,2,1,4096]{3,0,2,1:T(8,128)(2,1)S(1)}, u32[]{:S(2)}, u32[]{:S(2)}) %collective-permute-start) | collective-permute-done | bytes 1048608 | tf_op jit(solution)/shard_map/ppermute | solution.py:23
  27.2 1.8 collective-permute-done.1
  32.2 4.7 %copy.49 = bf16[64,3,1,4096]{0,1,2,3:T(4,128)(2,1)} copy(bf16[64,3,1,4096]{3,0,2,1:T(8,128)(2,1)S(1)} %pad_maximum_fusion.2) | data formatting | bytes 3145728 | tf_op jit(solution)/shard_map/stack | solution.py:44
  36.9 6.1 %reshape.243 = bf16[8,2,49152]{2,1,0:T(2,128)(2,1)S(1)} reshape(bf16[4096,1,3,64]{3,2,1,0:T(4,128)(2,1)} %bitcast.77) | data formatting | bytes 3145728
  43.0 48.1 %all_to_all.15 = bf16[8,2,49152]{2,1,0:T(2,128)(2,1)S(1)} all-to-all(bf16[8,2,49152]{2,1,0:T(2,128)(2,1)S(1)} %reshape.243), channel_id=1, replica_groups=mesh['frame'=8,'tile'=32] {'frame'}, dimensions={0} | all-to-all | bytes 3145728 | tf_op jit(solution)/shard_map/all_to_all | solution.py:63
  91.2 4.8 %reshape.244 = bf16[4096,1,3,64]{3,2,1,0:T(4,128)(2,1)} reshape(bf16[8,2,49152]{2,1,0:T(2,128)(2,1)S(1)} %all_to_all.15) | data formatting | bytes 3145728
  96.0 4.3 copy.67
  102.2 2.0 fusion.36
  104.7 109.7 %all-reduce.4.cloned.1.call-done = f32[512,512]{0,1:T(8,128)} async-done(((f32[512,512]{0,1:T(8,128)}), f32[512,512]{0,1:T(8,128)}) %all-reduce.4.cloned.1.call-update) | async-done | bytes 1048592 | tf_op jit(solution)/shard_map/psum | solution.py:10
  214.7 2.1 convert_element_type.26
  218.0 75.2 %all-reduce.6.cloned.1.call-done = f32[512,512]{0,1:T(8,128)} async-done(((f32[512,512]{0,1:T(8,128)}), f32[512,512]{0,1:T(8,128)}) %all-reduce.6.cloned.1.call-update) | async-done | bytes 1048592 | tf_op jit(solution)/shard_map/psum | solution.py:10
  295.1 11.7 %cholesky.104 = f32[128,128]{1,0:T(8,128)S(1)} custom-call(f32[128,128]{1,0:T(8,128)S(1)} %cholesky.266), custom_call_target="Cholesky" | custom-call | tf_op jit(solution)/shard_map/jit(cholesky)/cholesky | solution.py:70
  307.0 9.8 %custom-call.30 = f32[1,128,128]{1,2,0:T(8,128)S(1)} custom-call(f32[1,128,128]{2,1,0:T(8,128)S(1)} %get-tuple-element.45), custom_call_target="InvertDiagBlocksLowerTriangular" | custom-call | tf_op jit(solution)/shard_map/jit(cholesky)/cholesky | solution.py:70
  317.5 11.7 %cholesky.217 = f32[128,128]{1,0:T(8,128)S(1)} custom-call(f32[128,128]{1,0:T(8,128)S(1)} %cholesky.270), custom_call_target="Cholesky" | custom-call | tf_op jit(solution)/shard_map/jit(cholesky)/cholesky | solution.py:70
  330.4 10.0 %custom-call.31 = f32[1,128,128]{1,2,0:T(8,128)S(1)} custom-call(f32[1,128,128]{2,1,0:T(8,128)S(1)} %get-tuple-element.42), custom_call_target="InvertDiagBlocksLowerTriangular" | custom-call | tf_op jit(solution)/shard_map/jit(cholesky)/cholesky | solution.py:70
  341.1 11.7 %cholesky.238 = f32[128,128]{1,0:T(8,128)S(1)} custom-call(f32[128,128]{1,0:T(8,128)S(1)} %cholesky.275), custom_call_target="Cholesky" | custom-call | tf_op jit(solution)/shard_map/jit(cholesky)/cholesky | solution.py:70
  353.5 9.8 %custom-call.32 = f32[1,128,128]{1,2,0:T(8,128)S(1)} custom-call(f32[1,128,128]{2,1,0:T(8,128)S(1)} %get-tuple-element.39), custom_call_target="InvertDiagBlocksLowerTriangular" | custom-call | tf_op jit(solution)/shard_map/jit(cholesky)/cholesky | solution.py:70
  363.9 11.9 %cholesky.255 = f32[128,128]{1,0:T(8,128)S(1)} custom-call(f32[128,128]{1,0:T(8,128)S(1)} %convolution_subtract_fusion.5), custom_call_target="Cholesky" | custom-call | tf_op jit(solution)/shard_map/jit(cholesky)/cholesky | solution.py:70
  379.3 10.0 %while.1 = (s32[]{:T(128)}, f32[512,512]{1,0:T(8,128)S(1)}, s32[4,2]{0,1:T(2,128)S(1)}, f32[4,128,128]{2,1,0:T(8,128)}, s32[]{:T(128)}) while((s32[]{:T(128)}, f32[512,512]{1,0:T(8,128)S(1)}, s32[4,2]{0,1:T(2,128)S(1)}, f32[4,128,128]{2,1,0:T(8,128)}, s32[]{:T(128)}) %tuple.39), condition=%wide.while_cond, body=%wide.while_body.sunk | while | flops 2 | bytes 132705 | solution.py:72
  380.0 1.9 bitcast_dynamic-update-slice_fusion.2
  382.5 1.9 bitcast_dynamic-update-slice_fusion.2
  384.9 1.9 bitcast_dynamic-update-slice_fusion.2
  387.4 1.9 bitcast_dynamic-update-slice_fusion.2
  389.3 40.2 %custom-call.33 = f32[4,128,128]{1,2,0:T(8,128)S(1)} custom-call(f32[4,128,128]{2,1,0:T(8,128)} %get-tuple-element.9), custom_call_target="InvertDiagBlocksLowerTriangular" | custom-call | tf_op jit(solution)/shard_map/triangular_solve | solution.py:72
  431.2 2.1 convolution_subtract_fusion.2
  435.0 1.9 convolution_subtract_fusion
  438.6 3.4 fusion.1
  450.2 2.3 copy.60
  453.9 2.7 fusion.7
  (71 shorter events, 30.8 us)
Async XLA Ops:
  7.2 207.3 %all-reduce.4.cloned.1.call-start = ((), (), s32[]{:S(2)}) async-start(), calls=%async_computation.1 | async-start | bytes 2097152 | tf_op jit(solution)/shard_map/psum | solution.py:10
  9.0 18.2 %collective-permute-start = (bf16[64,2,1,4096]{3,0,2,1:T(8,128)(2,1)S(1)}, bf16[64,2,1,4096]{3,0,2,1:T(8,128)(2,1)S(1)}, u32[]{:S(2)}, u32[]{:S(2)}) collective-permute-start(bf16[64,2,1,4096]{3,0,2,1:T(8,128)(2,1)S(1)} %copy.46), channel_id=1, source_target_pairs={{0,1},{1,2},{2,3},{3,4},{4,5},{5,6},{6,7},{7,8},{8,9},{9,10},{10,1... | collective-permute-start | bytes 3145736 | tf_op jit(solution)/shard_map/ppermute | solution.py:23
  10.9 18.1 %collective-permute-start.1 = (bf16[64,2,1,4096]{3,0,2,1:T(8,128)(2,1)S(1)}, bf16[64,2,1,4096]{3,0,2,1:T(8,128)(2,1)S(1)}, u32[]{:S(2)}, u32[]{:S(2)}) collective-permute-start(bf16[64,2,1,4096]{3,0,2,1:T(8,128)(2,1)S(1)} %copy.46), channel_id=1, source_target_pairs={{1,0},{2,1},{3,2},{4,3},{5,4},{6,5},{7,6},{8,7},{9,8},{10,9},{11,1... | collective-permute-start | bytes 3145736 | tf_op jit(solution)/shard_map/ppermute | solution.py:24
  104.2 189.0 %all-reduce.6.cloned.1.call-start = ((), (), s32[]{:S(2)}) async-start(), calls=%async_computation.2 | async-start | bytes 2097152 | tf_op jit(solution)/shard_map/psum | solution.py:10
  293.2 1.7 copy-start.1
  389.3 40.2 %copy-start.3 = (f32[512,512]{1,0:T(8,128)}, f32[512,512]{1,0:T(8,128)S(1)}, u32[]{:S(2)}) copy-start(f32[512,512]{1,0:T(8,128)S(1)} %get-tuple-element.101) | copy-start | bytes 3145732
  429.5 1.6 copy-start.4
  431.2 3.8 copy-start
  444.3 4.3 copy-start.2
Sparse Core Ops, SparseCore 0:
  104.3 110.0 all-reduce.3
  216.9 76.2 all-reduce.5
